TPU v7x, 32 devices: a whole 2x2x4 slice. The times are simulated.
32 devices in a mesh: fsdp: 8 (over z, y), ctx: 2 (over x), tensor: 2 (over core).
Axes of the slice: x: 2, y: 2, z: 4, core: 2. Of those that a mesh axis runs over, the one named last changes fastest.
Arguments:
- block_input: bfloat16 [8, 1024, 1024], P('fsdp', 'ctx'), may hold values from -6 to 6
- operator_gain: bfloat16 [1024], P('fsdp'), may hold values from 0.5 to 1.5
- query_weight: bfloat16 [1024, 1024], P('fsdp', 'tensor'), may hold values from -0.1875 to 0.1875
- key_weight: bfloat16 [1024, 512], P('fsdp', 'tensor'), may hold values from -0.1875 to 0.1875
- value_weight: bfloat16 [1024, 512], P('fsdp', 'tensor'), may hold values from -0.1875 to 0.1875
- output_weight: bfloat16 [1024, 1024], P('tensor', 'fsdp'), may hold values from -0.75 to 0.75
- feedforward_gain: bfloat16 [1024], P('fsdp'), may hold values from 0.5 to 1.5
- gate_weight: bfloat16 [1024, 4608], P('fsdp', 'tensor'), may hold values from -0.1875 to 0.1875
- up_weight: bfloat16 [1024, 4608], P('fsdp', 'tensor'), may hold values from -0.1875 to 0.1875
- down_weight: bfloat16 [4608, 1024], P('tensor', 'fsdp'), may hold values from -0.09375 to 0.09375
- query_gain: bfloat16 [64], P('fsdp'), may hold values from 0.6 to 4
- key_gain: bfloat16 [64], P('fsdp'), may hold values from 0.6 to 4
- cotangent: bfloat16 [8, 1024, 1024], P('fsdp', 'ctx'), may hold values from -6 to 6
Outputs:
- block_output: bfloat16 [8, 1024, 1024], P('fsdp', 'ctx')
- input_grad: float32 [8, 1024, 1024], P('fsdp', 'ctx')
- operator_gain_grad: float32 [1024], P('fsdp')
- query_weight_grad: float32 [1024, 1024], P('fsdp', 'tensor')
- key_weight_grad: float32 [1024, 512], P('fsdp', 'tensor')
- value_weight_grad: float32 [1024, 512], P('fsdp', 'tensor')
- output_weight_grad: float32 [1024, 1024], P('tensor', 'fsdp')
- feedforward_gain_grad: float32 [1024], P('fsdp')
- gate_weight_grad: float32 [1024, 4608], P('fsdp', 'tensor')
- up_weight_grad: float32 [1024, 4608], P('fsdp', 'tensor')
- down_weight_grad: float32 [4608, 1024], P('tensor', 'fsdp')
- query_gain_grad: float32 [64], P('fsdp')
- key_gain_grad: float32 [64], P('fsdp')
All inputs are finite; a program needn't handle non-finite values.
Results may differ from a plain program's by a relative error of at most 0.024.
The roundings to bfloat16 on the way count: a program that leaves them out, or rounds other values in their place, can miss the bound.
Values may be sent and summed in bfloat16 or wider, within the bound.
A program may use at most 192 MiB of HBM per device.

v0:
```python
import jax
import jax.numpy as jnp
from jax import lax
from jax.sharding import PartitionSpec as P

EPS = 1e-05
THETA = 1000000.0


def rms_scale(values_in, gain):
    return (
        values_in * lax.rsqrt(jnp.mean(values_in * values_in, axis=-1, keepdims=True) + EPS) * gain
    )


def rotary_tables(positions, head_width):
    half_width = head_width // 2
    freqs = THETA ** (-jnp.arange(half_width).astype(jnp.float32) * 2.0 / head_width)
    angles = positions.astype(jnp.float32)[:, None] * freqs[None, :]
    return (jnp.cos(angles), jnp.sin(angles))


def rotate_halves(heads_in, cosine, sine):
    half_width = heads_in.shape[-1] // 2
    front_half = heads_in[..., :half_width]
    back_half = heads_in[..., half_width:]
    cos_rows = cosine[:, None, :]
    sin_rows = sine[:, None, :]
    return jnp.concatenate(
        [
            front_half * cos_rows - back_half * sin_rows,
            back_half * cos_rows + front_half * sin_rows,
        ],
        axis=-1,
    )


def head_prepare(raw, gain, cosine, sine):
    head_width = gain.shape[0]
    shaped = raw.reshape(raw.shape[:-1] + (raw.shape[-1] // head_width, head_width))
    return rotate_halves(rms_scale(shaped, gain), cosine, sine)


def swiglu(gate, upper):
    return jax.nn.silu(gate) * upper


def contract(left, right, left_dim, right_dim):
    return lax.dot_general(
        left, right, (((left_dim,), (right_dim,)), ((), ())), preferred_element_type=jnp.float32
    )


def block_scores(query_block, keys, query_pos, key_pos):
    scale = 1.0 / query_block.shape[-1] ** 0.5
    scores = (
        jnp.einsum("qhd,khd->hqk", query_block, keys, preferred_element_type=jnp.float32) * scale
    )
    allowed = key_pos[None, :] <= query_pos[:, None]
    return jnp.where(allowed[None, :, :], scores, -1e30)


def attend(queries, keys, values, positions):
    length = queries.shape[0]
    block_rows = min(512, length)
    outputs = []
    totals = []
    for start in range(0, length, block_rows):
        rows = slice(start, start + block_rows)
        scores = block_scores(queries[rows], keys, positions[rows], positions)
        peak = jnp.max(scores, axis=-1, keepdims=True)
        log_total = peak + jnp.log(jnp.sum(jnp.exp(scores - peak), axis=-1, keepdims=True))
        probs = jnp.exp(scores - log_total).astype(jnp.bfloat16)
        block_out = jnp.einsum("hqk,khd->qhd", probs, values, preferred_element_type=jnp.float32)
        outputs.append(block_out.astype(jnp.bfloat16))
        totals.append(log_total[..., 0])
    return (jnp.concatenate(outputs, axis=0), jnp.concatenate(totals, axis=1))


def attend_grad(queries, keys, values, outputs, totals, out_grad, positions):
    length = queries.shape[0]
    block_rows = min(512, length)
    scale = 1.0 / queries.shape[-1] ** 0.5
    key_acc = jnp.zeros(keys.shape, jnp.float32)
    value_acc = jnp.zeros(values.shape, jnp.float32)
    query_parts = []
    for start in range(0, length, block_rows):
        rows = slice(start, start + block_rows)
        query_block = queries[rows]
        scores = block_scores(query_block, keys, positions[rows], positions)
        probs = jnp.exp(scores - totals[:, rows][..., None])
        grad_block = out_grad[rows]
        value_acc = value_acc + jnp.einsum(
            "hqk,qhd->khd",
            probs.astype(jnp.bfloat16),
            grad_block,
            preferred_element_type=jnp.float32,
        )
        prob_grad = jnp.einsum(
            "qhd,khd->hqk", grad_block, values, preferred_element_type=jnp.float32
        )
        delta = jnp.sum(
            grad_block.astype(jnp.float32) * outputs[rows].astype(jnp.float32), axis=-1
        ).T
        score_grad = (probs * (prob_grad - delta[..., None])).astype(jnp.bfloat16)
        query_parts.append(
            (
                jnp.einsum("hqk,khd->qhd", score_grad, keys, preferred_element_type=jnp.float32)
                * scale
            ).astype(jnp.bfloat16)
        )
        key_acc = (
            key_acc
            + jnp.einsum(
                "hqk,qhd->khd", score_grad, query_block, preferred_element_type=jnp.float32
            )
            * scale
        )
    return (
        jnp.concatenate(query_parts, axis=0),
        key_acc.astype(jnp.bfloat16),
        value_acc.astype(jnp.bfloat16),
    )


def shift(array, axis_name, step):
    size = lax.axis_size(axis_name)
    return lax.ppermute(array, axis_name, [(i, (i + step) % size) for i in range(size)])


def around(array, axis_name, dim):
    size = lax.axis_size(axis_name)
    return jnp.concatenate(
        [array] + [shift(array, axis_name, step) for step in range(1, size)], axis=dim
    )


def group_rows(array):
    return around(around(array, "ctx", 1), "tensor", 1)


def sum_around(array, axis_name):
    size = lax.axis_size(axis_name)
    part = array.shape[1] // size
    total = array[:, :part].astype(jnp.float32)
    for step in range(1, size):
        piece = array[:, step * part : (step + 1) * part].astype(jnp.bfloat16)
        total = total + shift(piece, axis_name, -step).astype(jnp.float32)
    return total


def group_sum(array):
    return sum_around(sum_around(array, "tensor"), "ctx")


def in_order(array, axis_name, dim):
    size = lax.axis_size(axis_name)
    me = lax.axis_index(axis_name)
    width = array.shape[dim]
    shape = list(array.shape)
    shape[dim] = width * size
    out = jnp.zeros(shape, array.dtype)
    for step in range(size):
        piece = array if step == 0 else shift(array, axis_name, step)
        owner = lax.rem(me - step + size, size)
        out = lax.dynamic_update_slice_in_dim(out, piece, owner * width, dim)
    return out


def part_of(array, dim, count, start):
    return lax.dynamic_slice_in_dim(array, start, count, dim)


def shards(
    block_input,
    operator_gain,
    query_weight,
    key_weight,
    value_weight,
    output_weight,
    feedforward_gain,
    gate_weight,
    up_weight,
    down_weight,
    query_gain,
    key_gain,
    cotangent,
):
    bf16 = jnp.bfloat16
    f32 = jnp.float32
    fsdp = lax.axis_size("fsdp")
    ctx = lax.axis_size("ctx")
    tensor = lax.axis_size("tensor")
    me_f = lax.axis_index("fsdp")
    me_c = lax.axis_index("ctx")
    me_t = lax.axis_index("tensor")
    seqs, tok_here, width = block_input.shape
    quarter = tok_here // tensor
    tokens = tok_here * ctx
    rows = seqs * tokens
    gain_rows = query_gain.shape[0]
    head_width = gain_rows * fsdp
    heads_shard = query_weight.shape[1] // head_width
    kv_shard = key_weight.shape[1] // head_width
    spread = heads_shard // kv_shard
    heads = heads_shard // ctx
    kv = max(1, kv_shard // ctx)
    group = heads // kv
    copies = max(1, ctx // kv_shard)
    q_cols = heads * head_width
    kv_cols = kv * head_width
    kv_start = me_c * heads // spread * head_width
    hidden_units = gate_weight.shape[1] // ctx
    shard_rows = query_weight.shape[0]
    gains = jnp.stack(
        [
            operator_gain,
            feedforward_gain,
            jnp.pad(query_gain, (0, shard_rows - gain_rows)),
            jnp.pad(key_gain, (0, shard_rows - gain_rows)),
        ],
        axis=1,
    )
    attention_pack = jnp.concatenate(
        [
            part_of(query_weight, 1, q_cols, me_c * q_cols),
            part_of(key_weight, 1, kv_cols, kv_start),
            part_of(value_weight, 1, kv_cols, kv_start),
            part_of(output_weight, 0, q_cols, me_c * q_cols).T,
            jnp.pad(gains, ((0, 0), (0, 124))),
        ],
        axis=1,
    )
    gate_up_pack = jnp.concatenate(
        [
            part_of(gate_weight, 1, hidden_units, me_c * hidden_units),
            part_of(up_weight, 1, hidden_units, me_c * hidden_units),
        ],
        axis=1,
    )
    down_pack = part_of(down_weight, 0, hidden_units, me_c * hidden_units).T
    attention_full = lax.all_gather(attention_pack, "fsdp", axis=0, tiled=True)
    gate_up_full = lax.all_gather(gate_up_pack, "fsdp", axis=0, tiled=True)
    down_full = lax.all_gather(down_pack, "fsdp", axis=0, tiled=True)
    qkv_cols = q_cols + 2 * kv_cols
    qkv_full = attention_full[:, :qkv_cols]
    output_full = attention_full[:, qkv_cols : qkv_cols + q_cols]
    gains_full = attention_full[:, qkv_cols + q_cols :].astype(f32)
    operator_scale = gains_full[:, 0]
    feedforward_scale = gains_full[:, 1]
    query_scale = gains_full[:, 2].reshape(fsdp, shard_rows)[:, :gain_rows].reshape(-1)
    key_scale = gains_full[:, 3].reshape(fsdp, shard_rows)[:, :gain_rows].reshape(-1)
    own_input = part_of(block_input, 1, quarter, me_t * quarter)
    all_input = group_rows(own_input).reshape(rows, width)
    upstream_own = part_of(cotangent, 1, quarter, me_t * quarter)
    upstream = group_rows(upstream_own).reshape(rows, width)
    ctx_order = lax.rem(me_c - jnp.arange(ctx) + ctx, ctx)
    tensor_order = lax.rem(me_t - jnp.arange(tensor) + tensor, tensor)
    positions = (
        tensor_order[:, None, None] * quarter
        + ctx_order[None, :, None] * tok_here
        + jnp.arange(quarter)[None, None, :]
    ).reshape(tokens)
    cosine, sine = rotary_tables(positions, head_width)

    def prepare(raw, gain):
        return head_prepare(raw, gain, cosine, sine)

    normed_input = rms_scale(all_input.astype(f32), operator_scale).astype(bf16)
    qkv_raw = jnp.dot(normed_input, qkv_full, preferred_element_type=f32).reshape(seqs, tokens, -1)
    query_f32, query_back = jax.vjp(prepare, qkv_raw[..., :q_cols], query_scale)
    key_f32, key_back = jax.vjp(prepare, qkv_raw[..., q_cols : q_cols + kv_cols], key_scale)
    queries = query_f32.astype(bf16)
    keys = jnp.repeat(key_f32.astype(bf16), group, axis=2)
    values = jnp.repeat(
        qkv_raw[..., q_cols + kv_cols :].astype(bf16).reshape(seqs, tokens, kv, head_width),
        group,
        axis=2,
    )
    attended, totals = jax.vmap(attend, in_axes=(0, 0, 0, None))(queries, keys, values, positions)
    attended_rows = attended.reshape(rows, q_cols)
    attention_part = contract(attended_rows, output_full, 1, 1).reshape(seqs, tokens, width)
    own_f32 = own_input.astype(f32)
    hidden = own_f32 + group_sum(attention_part)
    norm_two, norm_two_back = jax.vjp(rms_scale, hidden, feedforward_scale)
    normed_hidden = group_rows(norm_two.astype(bf16)).reshape(rows, width)
    gate_up = jnp.dot(normed_hidden, gate_up_full, preferred_element_type=f32)
    act_f32, act_back = jax.vjp(swiglu, gate_up[:, :hidden_units], gate_up[:, hidden_units:])
    activation = act_f32.astype(bf16)
    act_grad = jnp.dot(upstream, down_full, preferred_element_type=f32)
    gate_grad, up_grad = act_back(act_grad)
    gate_up_grad = jnp.concatenate([gate_grad.astype(bf16), up_grad.astype(bf16)], axis=1)
    hidden_part = contract(gate_up_grad, gate_up_full, 1, 1).reshape(seqs, tokens, width)
    normed_hidden_grad = group_sum(hidden_part)
    down_grad = contract(upstream, activation, 0, 0).astype(bf16)
    down_share = lax.psum_scatter(down_grad, "fsdp", scatter_dimension=0, tiled=True)
    gate_up_weight_grad = contract(normed_hidden, gate_up_grad, 0, 0).astype(bf16)
    gate_up_share = lax.psum_scatter(gate_up_weight_grad, "fsdp", scatter_dimension=0, tiled=True)
    down_part = contract(activation, down_full, 1, 1).reshape(seqs, tokens, width)
    own_output = (hidden + group_sum(down_part)).astype(bf16)
    block_output = in_order(own_output, "tensor", 1)
    hidden_norm_grad, feedforward_gain_grad = norm_two_back(normed_hidden_grad)
    hidden_grad = upstream_own.astype(f32) + hidden_norm_grad
    hidden_grad_b = group_rows(hidden_grad.astype(bf16)).reshape(rows, width)
    output_weight_grad = contract(hidden_grad_b, attended_rows, 0, 0)
    attended_grad = (
        jnp.dot(hidden_grad_b, output_full, preferred_element_type=f32)
        .astype(bf16)
        .reshape(seqs, tokens, heads, head_width)
    )
    query_hgrad, key_hgrad, value_hgrad = jax.vmap(attend_grad, in_axes=(0, 0, 0, 0, 0, 0, None))(
        queries, keys, values, attended, totals, attended_grad, positions
    )

    def head_sum(grad):
        return grad.astype(f32).reshape(seqs, tokens, kv, group, head_width).sum(axis=3)

    query_pre, query_gain_grad = query_back(query_hgrad.astype(f32))
    key_pre, key_gain_grad = key_back(head_sum(key_hgrad))
    qkv_raw_grad = jnp.concatenate(
        [
            query_pre.astype(bf16).reshape(rows, q_cols),
            key_pre.astype(bf16).reshape(rows, kv_cols),
            head_sum(value_hgrad).astype(bf16).reshape(rows, kv_cols),
        ],
        axis=1,
    )
    input_part = contract(qkv_raw_grad, qkv_full, 1, 1).reshape(seqs, tokens, width)
    normed_input_grad = group_sum(input_part)
    qkv_weight_grad = contract(normed_input, qkv_raw_grad, 0, 0)
    attention_grad = jnp.concatenate([qkv_weight_grad, output_weight_grad], axis=1).astype(bf16)
    attention_share = lax.psum_scatter(attention_grad, "fsdp", scatter_dimension=0, tiled=True)
    _, norm_one_back = jax.vjp(rms_scale, own_f32, operator_scale)
    input_norm_grad, operator_gain_grad = norm_one_back(normed_input_grad)
    input_grad = in_order(hidden_grad + input_norm_grad, "tensor", 1)
    gain_sums = lax.psum(
        jnp.concatenate(
            [operator_gain_grad, feedforward_gain_grad, query_gain_grad, key_gain_grad]
        ),
        ("fsdp", "ctx", "tensor"),
    )
    operator_share = part_of(gain_sums, 0, shard_rows, me_f * shard_rows)
    feedforward_share = part_of(gain_sums, 0, shard_rows, width + me_f * shard_rows)
    query_gain_share = part_of(gain_sums, 0, gain_rows, 2 * width + me_f * gain_rows)
    key_gain_share = part_of(gain_sums, 0, gain_rows, 2 * width + head_width + me_f * gain_rows)

    def spread_cols(share):
        return in_order(share, "ctx", 1).astype(f32)

    def spread_heads(share):
        if copies == 1:
            return spread_cols(share)
        every = in_order(share, "ctx", 1).astype(f32)
        return (
            every.reshape(shard_rows, kv_shard, copies, head_width)
            .sum(axis=2)
            .reshape(shard_rows, -1)
        )

    return (
        block_output,
        input_grad,
        operator_share,
        spread_cols(attention_share[:, :q_cols]),
        spread_heads(attention_share[:, q_cols : q_cols + kv_cols]),
        spread_heads(attention_share[:, q_cols + kv_cols : qkv_cols]),
        in_order(attention_share[:, qkv_cols:].T, "ctx", 0).astype(f32),
        feedforward_share,
        spread_cols(gate_up_share[:, :hidden_units]),
        spread_cols(gate_up_share[:, hidden_units:]),
        in_order(down_share.T, "ctx", 0).astype(f32),
        query_gain_share,
        key_gain_share,
    )


def solution(mesh):
    in_specs = (
        P("fsdp", "ctx", None),
        P("fsdp"),
        P("fsdp", "tensor"),
        P("fsdp", "tensor"),
        P("fsdp", "tensor"),
        P("tensor", "fsdp"),
        P("fsdp"),
        P("fsdp", "tensor"),
        P("fsdp", "tensor"),
        P("tensor", "fsdp"),
        P("fsdp"),
        P("fsdp"),
        P("fsdp", "ctx", None),
    )
    out_specs = (
        P("fsdp", "ctx", None),
        P("fsdp", "ctx", None),
        P("fsdp"),
        P("fsdp", "tensor"),
        P("fsdp", "tensor"),
        P("fsdp", "tensor"),
        P("tensor", "fsdp"),
        P("fsdp"),
        P("fsdp", "tensor"),
        P("fsdp", "tensor"),
        P("tensor", "fsdp"),
        P("fsdp"),
        P("fsdp"),
    )
    return jax.shard_map(shards, mesh=mesh, in_specs=in_specs, out_specs=out_specs, check_vma=False)
```

profile of v0, /device:TPU:0, one launch (start us, length us, event | category | flops | bytes accessed | tf_op | source)
XLA Modules:
  0.0 509.7 jit_solution(16331534721619559554)
XLA Ops:
  13.8 2.9 collective-permute-start
  18.8 9.8 %collective-permute-done = bf16[1,256,1024]{2,1,0:T(8,128)(2,1)S(1)} collective-permute-done((bf16[1,256,1024]{2,1,0:T(8,128)(2,1)S(1)}, bf16[1,256,1024]{2,1,0:T(8,128)(2,1)S(1)}, u32[]{:S(2)}, u32[]{:S(2)}) %collective-permute-start) | collective-permute-done | bytes 524320 | tf_op jit(solution)/shard_map/ppermute | solution.py:128
  31.9 31.1 %all-gather.4.cloned.1.call-done = bf16[1024,896]{0,1:T(8,128)(2,1)} async-done(((bf16[128,896]{0,1:T(8,128)(2,1)}), bf16[1024,896]{0,1:T(8,128)(2,1)}) %all-gather.4.cloned.1.call-update) | async-done | bytes 1835024 | tf_op jit(solution)/shard_map/all_gather | solution.py:242
  64.1 3.1 convolution_bitcast_fusion.3
  76.1 2.6 exponential_reduce_fusion.1
  80.4 2.4 exponential_reduce_fusion
  99.4 12.4 %collective-permute-done.3 = bf16[1,256,1024]{2,1,0:T(8,128)(2,1)S(1)} collective-permute-done((bf16[1,256,1024]{2,1,0:T(8,128)(2,1)S(1)}, bf16[1,256,1024]{2,1,0:T(8,128)(2,1)S(1)}, u32[]{:S(2)}, u32[]{:S(2)}) %collective-permute-start.3) | collective-permute-done | bytes 524320 | tf_op jit(solution)/shard_map/ppermute | solution.py:128
  113.9 11.7 %collective-permute-done.4 = bf16[1,256,1024]{2,1,0:T(8,128)(2,1)S(1)} collective-permute-done((bf16[1,256,1024]{2,1,0:T(8,128)(2,1)S(1)}, bf16[1,256,1024]{2,1,0:T(8,128)(2,1)S(1)}, u32[]{:S(2)}, u32[]{:S(2)}) %collective-permute-start.4) | collective-permute-done | bytes 524320 | tf_op jit(solution)/shard_map/ppermute | solution.py:128
  128.1 12.8 %collective-permute-done.9 = bf16[1,256,1024]{2,1,0:T(8,128)(2,1)S(1)} collective-permute-done((bf16[1,256,1024]{2,1,0:T(8,128)(2,1)S(1)}, bf16[1,256,1024]{2,1,0:T(8,128)(2,1)S(1)}, u32[]{:S(2)}, u32[]{:S(2)}) %collective-permute-start.9) | collective-permute-done | bytes 524320 | tf_op jit(solution)/shard_map/ppermute | solution.py:128
  143.3 11.5 %fusion.36 = f32[1024,2304]{1,0:T(8,128)} fusion(bf16[1024,2304]{1,0:T(8,128)(2,1)} %all-gather.6.cloned.1.call-done, bf16[1,512,1024]{2,1,0:T(8,128)(2,1)} %collective-permute-done.5, bf16[1,256,1024]{2,1,0:T(8,128)(2,1)} %copy-done.49, bf16[1,256,1024]{2,1,0:T(8,128)(2,1)S(1)} %multiply_convert_fusion.4), kind=kOutput, calls=%fused_computation.111 | convolution fusion | flops 4838129664 | bytes 16252928 | tf_op jit(solution)/shard_map/dot_general | solution.py:287
  154.9 42.4 %all-gather.8.cloned.1.call-done = bf16[1024,1152]{0,1:T(8,128)(2,1)} async-done(((bf16[128,1152]{0,1:T(8,128)(2,1)}), bf16[1024,1152]{0,1:T(8,128)(2,1)}) %all-gather.8.cloned.1.call-update) | async-done | bytes 2359312 | tf_op jit(solution)/shard_map/all_gather | solution.py:244
  197.3 9.1 %fusion.6 = (bf16[1024,1152]{1,0:T(8,128)(2,1)S(1)}, bf16[1024,1152]{1,0:T(8,128)(2,1)S(1)}, bf16[1024,1152]{1,0:T(8,128)(2,1)S(1)}) fusion(f32[1024,2304]{1,0:T(8,128)} %fusion.36, bf16[1024,1152]{0,1:T(8,128)(2,1)} %all-gather.8.cloned.1.call-done, bf16[1,512,1024]{2,1,0:T(8,128)(2,1)} %collective-permute-done.10, bf16[1,256,1024]{2,1,0:T(8,128)(2,1)} %copy-done.53, ...), kind=kOutput, calls=%fused_computation.18 | convolution fusion | flops 2441084928 | bytes 20971520 | tf_op jit(solution)/shard_map/dot_general | solution.py:290
  206.4 5.1 fusion.12
  211.7 2.6 collective-permute-done.11
  216.3 12.5 %collective-permute-done.12 = bf16[1,256,1024]{2,1,0:T(8,128)(2,1)S(1)} collective-permute-done((bf16[1,256,1024]{2,1,0:T(8,128)(2,1)S(1)}, bf16[1,256,1024]{2,1,0:T(8,128)(2,1)S(1)}, u32[]{:S(2)}, u32[]{:S(2)}) %collective-permute-start.12) | collective-permute-done | bytes 524320 | tf_op jit(solution)/shard_map/ppermute | solution.py:128
  232.1 11.6 %collective-permute-done.13 = bf16[1,256,1024]{2,1,0:T(8,128)(2,1)S(1)} collective-permute-done((bf16[1,256,1024]{2,1,0:T(8,128)(2,1)S(1)}, bf16[1,256,1024]{2,1,0:T(8,128)(2,1)S(1)}, u32[]{:S(2)}, u32[]{:S(2)}) %collective-permute-start.13) | collective-permute-done | bytes 524320 | tf_op jit(solution)/shard_map/ppermute | solution.py:128
  245.6 5.6 %convolution_convert_fusion.1 = bf16[1024,1152]{1,0:T(8,128)(2,1)} fusion(bf16[1024,1152]{1,0:T(8,128)(2,1)S(1)} %get-tuple-element.35, bf16[1,512,1024]{2,1,0:T(8,128)(2,1)} %collective-permute-done.10, bf16[1,256,1024]{2,1,0:T(8,128)(2,1)S(1)} %copy-done.54, bf16[1,256,1024]{2,1,0:T(8,128)(2,1)S(1)} %constant_dynamic-slice_fusion), kind=kOutput, calls=%fused_computation.27 | convolution fusion | flops 2423390208 | bytes 6815744 | tf_op jit(solution)/shard_map/dot_general | solution.py:49
  251.3 2.6 convolution_convert_fusion.4
  254.2 5.5 %multiply_convert_fusion.1 = bf16[4,512,1024]{2,1,0:T(8,128)(2,1)S(1)} fusion(f32[4,512,1024]{2,1,0:T(8,128)} %copy-done.2, f32[4,512]{1,0:T(4,128)S(1)} %bitcast.212, f32[4,512]{1,0:T(4,128)S(1)} %log_add_fusion.1, pred[512,1024]{1,0:T(8,128)(4,1)S(1)} %copy-done.14, bf16[1024,4,64]{0,2,1:T(8,128)(2,1)S(1)} %bitcast.186, ...), kind=kOutput, calls=%fused_computation.1 | convolution fusion | flops 281018368 | bytes 13910016 | tf_op jit(solution)/shard_map/vmap(qhd,khd->hqk)/dot_general | solution.py:99
  259.8 3.5 multiply_convert_fusion
  270.7 3.8 fusion.22
  277.1 2.5 convolution_convert_fusion.3
  287.7 2.6 copy.48
  290.6 10.1 %convolution_convert_fusion = bf16[1024,2304]{1,0:T(8,128)(2,1)} fusion(bf16[1024,1152]{1,0:T(8,128)(2,1)} %copy-done.66, bf16[1024,1152]{1,0:T(8,128)(2,1)} %copy-done.65, bf16[1,512,1024]{2,1,0:T(8,128)(2,1)} %collective-permute-done.5, bf16[1,256,1024]{2,1,0:T(8,128)(2,1)S(1)} %copy-done.50, bf16[1,256,1024]{2,1,0:T(8,128)(2,1)S(1)} %copy-done.31), kind=kOutput, calls=%fused_computation.11 | convolution fusion | flops 4849926144 | bytes 11534336 | tf_op jit(solution)/shard_map/dot_general | solution.py:49
  300.7 5.4 %convolution_bitcast_fusion.2 = f32[1,1024,1024]{2,1,0:T(8,128)S(1)} fusion(bf16[1024,1152]{1,0:T(8,128)(2,1)} %copy-done.67, bf16[1024,1152]{0,1:T(8,128)(2,1)} %all-gather.8.cloned.1.call-done), kind=kOutput, calls=%fused_computation.32 | convolution fusion | flops 2415919104 | bytes 8912896 | tf_op jit(solution)/shard_map/dot_general | solution.py:49
  313.4 2.4 slice_add_fusion.2
  318.7 12.0 %collective-permute-done.7 = bf16[1,256,1024]{2,1,0:T(8,128)(2,1)S(1)} collective-permute-done((bf16[1,256,1024]{2,1,0:T(8,128)(2,1)S(1)}, bf16[1,256,1024]{2,1,0:T(8,128)(2,1)S(1)}, u32[]{:S(2)}, u32[]{:S(2)}) %collective-permute-start.7) | collective-permute-done | bytes 524320 | tf_op jit(solution)/shard_map/ppermute | solution.py:128
  332.0 9.5 %collective-permute-done.16 = bf16[1,256,1024]{2,1,0:T(8,128)(2,1)S(1)} collective-permute-done((bf16[1,256,1024]{2,1,0:T(8,128)(2,1)S(1)}, bf16[1,256,1024]{2,1,0:T(8,128)(2,1)S(1)}, u32[]{:S(2)}, u32[]{:S(2)}) %collective-permute-start.16) | collective-permute-done | bytes 524320 | tf_op jit(solution)/shard_map/ppermute | solution.py:128
  348.2 40.7 %psum.7 = f32[2176]{0:T(1024)S(1)} all-reduce(f32[2176]{0:T(1024)S(1)} %concatenate.102), channel_id=1, replica_groups=mesh['fsdp'=8,'ctx'=2,'tensor'=2] {'fsdp','ctx','tensor'}, use_global_device_ids=true, to_apply=%region_21.22 | all-reduce | flops 2176 | bytes 17408 | tf_op jit(solution)/shard_map/psum | solution.py:336
  405.0 80.4 %reduce-scatter.6.cloned.1.call-done = bf16[128,2304]{1,0:T(8,128)(2,1)} async-done(((bf16[1024,2304]{1,0:T(8,128)(2,1)}), bf16[128,2304]{1,0:T(8,128)(2,1)}) %reduce-scatter.6.cloned.1.call-update) | async-done | bytes 589840 | tf_op jit(solution)/shard_map/reduce_scatter | solution.py:298
  489.7 6.8 %collective-permute-done.23 = bf16[128,1152]{1,0:T(8,128)(2,1)S(1)} collective-permute-done((bf16[128,1152]{1,0:T(8,128)(2,1)S(1)}, bf16[128,1152]{1,0:T(8,128)(2,1)S(1)}, u32[]{:S(2)}, u32[]{:S(2)}) %collective-permute-start.23) | collective-permute-done | bytes 294944 | tf_op jit(solution)/shard_map/ppermute | solution.py:128
  497.7 3.8 collective-permute-done.22
  (348 shorter events, 112.9 us)
Async XLA Ops:
  7.2 55.8 %all-gather.4.cloned.1.call-start = ((), (), s32[]{:S(2)}) async-start(), calls=%async_computation.3 | async-start | bytes 2064384 | tf_op jit(solution)/shard_map/all_gather | solution.py:242
  12.5 130.9 %all-gather.6.cloned.1.call-start = ((), (), s32[]{:S(2)}) async-start(), calls=%async_computation.4 | async-start | bytes 5308416 | tf_op jit(solution)/shard_map/all_gather | solution.py:243
  13.8 14.9 %collective-permute-start = (bf16[1,256,1024]{2,1,0:T(8,128)(2,1)S(1)}, bf16[1,256,1024]{2,1,0:T(8,128)(2,1)S(1)}, u32[]{:S(2)}, u32[]{:S(2)}) collective-permute-start(bf16[1,256,1024]{2,1,0:T(8,128)(2,1)S(1)} %get-tuple-element.28), channel_id=1, source_target_pairs={{0,2},{2,0},{1,3},{3,1},{4,6},{6,4},{5,7},{7,5},{8,10},{10,8},{9,1... | collective-permute-start | bytes 1572872 | tf_op jit(solution)/shard_map/ppermute | solution.py:128
  18.7 178.6 %all-gather.8.cloned.1.call-start = ((), (), s32[]{:S(2)}) async-start(), calls=%async_computation.5 | async-start | bytes 2654208 | tf_op jit(solution)/shard_map/all_gather | solution.py:244
  28.7 2.7 collective-permute-start.1
  92.9 2.9 collective-permute-start.2
  93.7 251.7 %reduce-scatter.8.cloned.1.call-start = ((), (), s32[]{:S(2)}) async-start(), calls=%async_computation.7 | async-start | bytes 2654208 | tf_op jit(solution)/shard_map/reduce_scatter | solution.py:296
  97.8 14.0 %collective-permute-start.3 = (bf16[1,256,1024]{2,1,0:T(8,128)(2,1)S(1)}, bf16[1,256,1024]{2,1,0:T(8,128)(2,1)S(1)}, u32[]{:S(2)}, u32[]{:S(2)}) collective-permute-start(bf16[1,256,1024]{2,1,0:T(8,128)(2,1)S(1)} %slice.359), channel_id=1, source_target_pairs={{0,2},{2,0},{1,3},{3,1},{4,6},{6,4},{5,7},{7,5},{8,10},{10,8},{9,1... | collective-permute-start | bytes 1572872 | tf_op jit(solution)/shard_map/ppermute | solution.py:128
  112.3 13.3 %collective-permute-start.4 = (bf16[1,256,1024]{2,1,0:T(8,128)(2,1)S(1)}, bf16[1,256,1024]{2,1,0:T(8,128)(2,1)S(1)}, u32[]{:S(2)}, u32[]{:S(2)}) collective-permute-start(bf16[1,256,1024]{2,1,0:T(8,128)(2,1)S(1)} %multiply_convert_fusion.4), channel_id=1, source_target_pairs={{0,2},{2,0},{1,3},{3,1},{4,6},{6,4},{5,7},{7,5},{8,10},{10,8},{9,1... | collective-permute-start | bytes 1572872 | tf_op jit(solution)/shard_map/ppermute | solution.py:128
  126.4 16.3 %collective-permute-start.5 = (bf16[1,512,1024]{2,1,0:T(8,128)(2,1)S(1)}, bf16[1,512,1024]{2,1,0:T(8,128)(2,1)}, u32[]{:S(2)}, u32[]{:S(2)}) collective-permute-start(bf16[1,512,1024]{2,1,0:T(8,128)(2,1)S(1)} %pad_maximum_fusion.7), channel_id=1, source_target_pairs={{0,1},{1,0},{2,3},{3,2},{4,5},{5,4},{6,7},{7,6},{8,9},{9,8},{10,11... | collective-permute-start | bytes 3145736 | tf_op jit(solution)/shard_map/ppermute | solution.py:128
  126.5 14.4 %collective-permute-start.9 = (bf16[1,256,1024]{2,1,0:T(8,128)(2,1)S(1)}, bf16[1,256,1024]{2,1,0:T(8,128)(2,1)S(1)}, u32[]{:S(2)}, u32[]{:S(2)}) collective-permute-start(bf16[1,256,1024]{2,1,0:T(8,128)(2,1)S(1)} %constant_dynamic-slice_fusion), channel_id=1, source_target_pairs={{0,2},{2,0},{1,3},{3,1},{4,6},{6,4},{5,7},{7,5},{8,10},{10,8},{9,1... | collective-permute-start | bytes 1572872 | tf_op jit(solution)/shard_map/ppermute | solution.py:128
  142.7 12.2 %collective-permute-start.10 = (bf16[1,512,1024]{2,1,0:T(8,128)(2,1)}, bf16[1,512,1024]{2,1,0:T(8,128)(2,1)}, u32[]{:S(2)}, u32[]{:S(2)}) collective-permute-start(bf16[1,512,1024]{2,1,0:T(8,128)(2,1)} %pad_maximum_fusion.8), channel_id=1, source_target_pairs={{0,1},{1,0},{2,3},{3,2},{4,5},{5,4},{6,7},{7,6},{8,9},{9,8},{10,11... | collective-permute-start | bytes 3145736 | tf_op jit(solution)/shard_map/ppermute | solution.py:128
  211.7 2.7 collective-permute-start.11
  214.8 14.0 %collective-permute-start.12 = (bf16[1,256,1024]{2,1,0:T(8,128)(2,1)S(1)}, bf16[1,256,1024]{2,1,0:T(8,128)(2,1)S(1)}, u32[]{:S(2)}, u32[]{:S(2)}) collective-permute-start(bf16[1,256,1024]{2,1,0:T(8,128)(2,1)S(1)} %slice.357), channel_id=1, source_target_pairs={{0,2},{2,0},{1,3},{3,1},{4,6},{6,4},{5,7},{7,5},{8,10},{10,8},{9,1... | collective-permute-start | bytes 1572872 | tf_op jit(solution)/shard_map/ppermute | solution.py:128
  230.6 13.1 %collective-permute-start.13 = (bf16[1,256,1024]{2,1,0:T(8,128)(2,1)S(1)}, bf16[1,256,1024]{2,1,0:T(8,128)(2,1)S(1)}, u32[]{:S(2)}, u32[]{:S(2)}) collective-permute-start(bf16[1,256,1024]{2,1,0:T(8,128)(2,1)S(1)} %get-tuple-element.25), channel_id=1, source_target_pairs={{0,2},{2,0},{1,3},{3,1},{4,6},{6,4},{5,7},{7,5},{8,10},{10,8},{9,1... | collective-permute-start | bytes 1572872 | tf_op jit(solution)/shard_map/ppermute | solution.py:128
  245.6 5.8 %collective-permute-start.14 = (bf16[1,512,1024]{2,1,0:T(8,128)(2,1)}, bf16[1,512,1024]{2,1,0:T(8,128)(2,1)}, u32[]{:S(2)}, u32[]{:S(2)}) collective-permute-start(bf16[1,512,1024]{2,1,0:T(8,128)(2,1)} %pad_maximum_fusion.9), channel_id=1, source_target_pairs={{0,1},{1,0},{2,3},{3,2},{4,5},{5,4},{6,7},{7,6},{8,9},{9,8},{10,11... | collective-permute-start | bytes 3145736 | tf_op jit(solution)/shard_map/ppermute | solution.py:128
  251.3 141.6 %reduce-scatter.10.cloned.1.call-start = ((), (), s32[]{:S(2)}) async-start(), calls=%async_computation.8 | async-start | bytes 1769472
  290.3 195.1 %reduce-scatter.6.cloned.1.call-start = ((), (), s32[]{:S(2)}) async-start(), calls=%async_computation.6 | async-start | bytes 5308416 | tf_op jit(solution)/shard_map/reduce_scatter | solution.py:298
  308.4 5.0 collective-permute-start.6
  313.4 4.0 collective-permute-start.15
  315.9 14.9 %collective-permute-start.7 = (bf16[1,256,1024]{2,1,0:T(8,128)(2,1)S(1)}, bf16[1,256,1024]{2,1,0:T(8,128)(2,1)S(1)}, u32[]{:S(2)}, u32[]{:S(2)}) collective-permute-start(bf16[1,256,1024]{2,1,0:T(8,128)(2,1)S(1)} %slice.358), channel_id=1, source_target_pairs={{0,2},{2,0},{1,3},{3,1},{4,6},{6,4},{5,7},{7,5},{8,10},{10,8},{9,1... | collective-permute-start | bytes 1572872 | tf_op jit(solution)/shard_map/ppermute | solution.py:128
  318.0 23.5 %collective-permute-start.16 = (bf16[1,256,1024]{2,1,0:T(8,128)(2,1)S(1)}, bf16[1,256,1024]{2,1,0:T(8,128)(2,1)S(1)}, u32[]{:S(2)}, u32[]{:S(2)}) collective-permute-start(bf16[1,256,1024]{2,1,0:T(8,128)(2,1)S(1)} %slice.356), channel_id=1, source_target_pairs={{0,2},{2,0},{1,3},{3,1},{4,6},{6,4},{5,7},{7,5},{8,10},{10,8},{9,1... | collective-permute-start | bytes 1572872 | tf_op jit(solution)/shard_map/ppermute | solution.py:128
  331.9 11.6 %collective-permute-start.8 = (bf16[1,256,1024]{2,1,0:T(8,128)(2,1)}, bf16[1,256,1024]{2,1,0:T(8,128)(2,1)}, u32[]{:S(2)}, u32[]{:S(2)}) collective-permute-start(bf16[1,256,1024]{2,1,0:T(8,128)(2,1)} %get-tuple-element.30), channel_id=1, source_target_pairs={{0,1},{1,0},{2,3},{3,2},{4,5},{5,4},{6,7},{7,6},{8,9},{9,8},{10,11... | collective-permute-start | bytes 1572872 | tf_op jit(solution)/shard_map/ppermute | solution.py:128
  343.5 48.0 %collective-permute-start.17 = (f32[1,256,1024]{2,1,0:T(8,128)}, f32[1,256,1024]{2,1,0:T(8,128)}, u32[]{:S(2)}, u32[]{:S(2)}) collective-permute-start(f32[1,256,1024]{2,1,0:T(8,128)} %get-tuple-element.24), channel_id=1, source_target_pairs={{0,1},{1,0},{2,3},{3,2},{4,5},{5,4},{6,7},{7,6},{8,9},{9,8},{10,11... | collective-permute-start | bytes 3145736 | tf_op jit(solution)/shard_map/ppermute | solution.py:128
  346.6 43.6 %collective-permute-start.24 = (bf16[1152,128]{0,1:T(8,128)(2,1)}, bf16[1152,128]{0,1:T(8,128)(2,1)S(1)}, u32[]{:S(2)}, u32[]{:S(2)}) collective-permute-start(bf16[1152,128]{0,1:T(8,128)(2,1)} %bitcast.196), channel_id=1, source_target_pairs={{0,2},{2,0},{1,3},{3,1},{4,6},{6,4},{5,7},{7,5},{8,10},{10,8},{9,1... | collective-permute-start | bytes 884744 | tf_op jit(solution)/shard_map/ppermute | solution.py:128
  392.9 104.8 %copy-start.27 = (f32[1,512,1024]{2,1,0:T(8,128)}, f32[1,512,1024]{2,1,0:T(8,128)S(1)}, u32[]{:S(2)}) copy-start(f32[1,512,1024]{2,1,0:T(8,128)S(1)} %constant_dynamic-update-slice_fusion.17) | copy-start | bytes 6291460
  394.1 8.9 %collective-permute-start.21 = (bf16[256,128]{1,0:T(8,128)(2,1)S(1)}, bf16[256,128]{1,0:T(8,128)(2,1)S(1)}, u32[]{:S(2)}, u32[]{:S(2)}) collective-permute-start(bf16[256,128]{1,0:T(8,128)(2,1)S(1)} %bitcast.199), channel_id=1, source_target_pairs={{0,2},{2,0},{1,3},{3,1},{4,6},{6,4},{5,7},{7,5},{8,10},{10,8},{9,1... | collective-permute-start | bytes 196616 | tf_op jit(solution)/shard_map/ppermute | solution.py:128
  397.4 4.0 collective-permute-start.20
  397.6 4.6 collective-permute-start.19
  399.8 4.3 collective-permute-start.18
  486.6 9.9 %collective-permute-start.23 = (bf16[128,1152]{1,0:T(8,128)(2,1)S(1)}, bf16[128,1152]{1,0:T(8,128)(2,1)S(1)}, u32[]{:S(2)}, u32[]{:S(2)}) collective-permute-start(bf16[128,1152]{1,0:T(8,128)(2,1)S(1)} %get-tuple-element.44), channel_id=1, source_target_pairs={{0,2},{2,0},{1,3},{3,1},{4,6},{6,4},{5,7},{7,5},{8,10},{10,8},{9,1... | collective-permute-start | bytes 884744 | tf_op jit(solution)/shard_map/ppermute | solution.py:128
  488.1 13.3 %collective-permute-start.22 = (bf16[128,1152]{1,0:T(8,128)(2,1)S(1)}, bf16[128,1152]{1,0:T(8,128)(2,1)S(1)}, u32[]{:S(2)}, u32[]{:S(2)}) collective-permute-start(bf16[128,1152]{1,0:T(8,128)(2,1)S(1)} %get-tuple-element.46), channel_id=1, source_target_pairs={{0,2},{2,0},{1,3},{3,1},{4,6},{6,4},{5,7},{7,5},{8,10},{10,8},{9,1... | collective-permute-start | bytes 884744 | tf_op jit(solution)/shard_map/ppermute | solution.py:128
  (73 other events, 787.9 us)
Sparse Core Ops, SparseCore 0:
  12.6 50.3 all-gather.3
  65.8 77.4 all-gather.5
  145.4 51.8 all-gather.7
  251.4 67.9 reduce-scatter.7
  322.6 64.6 reduce-scatter.9
  390.8 94.5 reduce-scatter.5
where the time goes:
time: 516 us; the launch traced here: 510 us
  waiting for transfers between devices  264 us (51%)
  matrix products  89.8 us (17%)
  blocking collectives  40.7 us (8%)
  other arithmetic  38.9 us (8%)
  local copies, waits for them, and re-layouts  38.3 us (7%)
  starting transfers between devices  22.3 us (4%)
  between operations  15.9 us (3%)
    ppermute x25, waiting for transfers between devices, shift(): lax.ppermute(array, axis_name, [(i, (i + step) % size) for i in range(siz...  109 us
    reduce_scatter x1, waiting for transfers between devices, shards(): lax.psum_scatter(gate_up_weight_grad, 'fsdp', scatter_dimension=0, tiled=...  80.4 us
    all_gather x1, waiting for transfers between devices, shards(): down_full = lax.all_gather(down_pack, 'fsdp', axis=0, tiled=True)  42.4 us
    psum x1, blocking collectives, shards(): lax.psum(jnp.concatenate([operator_gain_grad, feedforward_gain_grad, quer...  40.7 us
    dot_general x8, matrix products, contract(): lax.dot_general(left, right, (((left_dim,), (right_dim,)), ((), ())), pre...  33.3 us
    all_gather x1, waiting for transfers between devices, shards(): attention_full = lax.all_gather(attention_pack, 'fsdp', axis=0, tiled=True)  31.1 us
    ppermute x25, starting transfers between devices, shift(): lax.ppermute(array, axis_name, [(i, (i + step) % size) for i in range(siz...  21.9 us
    unnamed x164, local copies, waits for them, and re-layouts  15.2 us
  transfers between devices with their start and end apart: 31, of which 19 were waited for; matrix products, arithmetic and copies ran while one was open for 26% of the time, Pallas kernels for 0%

commit v1 on v0

--- a/solution.py
+++ b/solution.py
@@ -5,6 +5,19 @@
 
 EPS = 1e-05
 THETA = 1000000.0
+
+
+def ring_gather(x, axis, dim):
+    ways = lax.axis_size(axis)
+    up = [(d, (d + 1) % ways) for d in range(ways)]
+    down = [(d, (d - 1) % ways) for d in range(ways)]
+    earlier, later = ([x], [x])
+    for _ in range(ways // 2):
+        earlier.append(lax.ppermute(earlier[-1], axis, up))
+    for _ in range((ways - 1) // 2):
+        later.append(lax.ppermute(later[-1], axis, down))
+    line = jnp.concatenate([*earlier[::-1], *later[1:]], axis=dim)
+    return jnp.roll(line, (lax.axis_index(axis) - ways // 2) * x.shape[dim], axis=dim)
 
 
 def rms_scale(values_in, gain):
@@ -239,7 +252,7 @@
         axis=1,
     )
     down_pack = part_of(down_weight, 0, hidden_units, me_c * hidden_units).T
-    attention_full = lax.all_gather(attention_pack, "fsdp", axis=0, tiled=True)
+    attention_full = ring_gather(attention_pack, "fsdp", 0)
     gate_up_full = lax.all_gather(gate_up_pack, "fsdp", axis=0, tiled=True)
     down_full = lax.all_gather(down_pack, "fsdp", axis=0, tiled=True)
     qkv_cols = q_cols + 2 * kv_cols

time: 516 us -> 484 us (0.938)
  waiting for transfers between devices: 264 us -> 206 us
  starting transfers between devices: 22.3 us -> 39.6 us
  local copies, waits for them, and re-layouts: 38.3 us -> 45.5 us
    all_gather x1, waiting for transfers between devices: 42.4 us -> 1.75 us  [shards(): down_full = lax.all_gather(down_pack, 'fsdp', axis=0, tiled=True)]
    all_gather x1 -> x0, waiting for transfers between devices: 31.1 us -> none  [shards(): attention_full = lax.all_gather(attention_pack, 'fsdp', axis=0, tiled=True)]
    ppermute x0 -> x7, waiting for transfers between devices: none -> 25.5 us  [the longest x4 25.5 us: ring_gather(): earlier.append(lax.ppermute(earlier[-1], axis, up))]
    ppermute x0 -> x7, starting transfers between devices: none -> 19.2 us  [the longest x3 11.6 us: ring_gather(): later.append(lax.ppermute(later[-1], axis, down))]
    unnamed x164 -> x183, local copies, waits for them, and re-layouts: 15.2 us -> 24.9 us
    ppermute x25, waiting for transfers between devices: 109 us -> 99.4 us  [shift(): lax.ppermute(array, axis_name, [(i, (i + step) % size) for i in range(siz...]
  transfers between devices with their start and end apart: 31 -> 37, of which waited for: 19 -> 19; matrix products, arithmetic and copies ran while one was open for 26% -> 29% of each run, Pallas kernels for 0% -> 0%
where the time goes in v1:
time: 484 us; the launch traced here: 476 us
  waiting for transfers between devices  206 us (43%)
  matrix products  91.7 us (19%)
  local copies, waits for them, and re-layouts  45.5 us (9%)
  blocking collectives  41.5 us (9%)
  starting transfers between devices  39.6 us (8%)
  other arithmetic  36.4 us (8%)
  between operations  15.8 us (3%)
    ppermute x25, waiting for transfers between devices, shift(): lax.ppermute(array, axis_name, [(i, (i + step) % size) for i in range(siz...  99.4 us
    reduce_scatter x1, waiting for transfers between devices, shards(): lax.psum_scatter(gate_up_weight_grad, 'fsdp', scatter_dimension=0, tiled=...  78.8 us
    psum x1, blocking collectives, shards(): lax.psum(jnp.concatenate([operator_gain_grad, feedforward_gain_grad, quer...  41.5 us
    dot_general x8, matrix products, contract(): lax.dot_general(left, right, (((left_dim,), (right_dim,)), ((), ())), pre...  35.2 us
    ppermute x4, waiting for transfers between devices, ring_gather(): earlier.append(lax.ppermute(earlier[-1], axis, up))  25.5 us
    unnamed x183, local copies, waits for them, and re-layouts  24.9 us
    ppermute x25, starting transfers between devices, shift(): lax.ppermute(array, axis_name, [(i, (i + step) % size) for i in range(siz...  20 us
    ppermute x3, starting transfers between devices, ring_gather(): later.append(lax.ppermute(later[-1], axis, down))  11.6 us
  transfers between devices with their start and end apart: 37, of which 19 were waited for; matrix products, arithmetic and copies ran while one was open for 29% of the time, Pallas kernels for 0%

profile of v1, /device:TPU:0, one launch (start us, length us, event | category | flops | bytes accessed | tf_op | source)
XLA Modules:
  0.0 476.1 jit_solution(2632232070321642448)
XLA Ops:
  11.8 3.0 collective-permute-start.2
  14.8 3.1 collective-permute-start.6
  27.1 8.6 %collective-permute-done.3 = bf16[128,896]{0,1:T(8,128)(2,1)S(1)} collective-permute-done((bf16[128,896]{0,1:T(8,128)(2,1)S(1)}, bf16[128,896]{0,1:T(8,128)(2,1)S(1)}, u32[]{:S(2)}, u32[]{:S(2)}) %collective-permute-start.3) | collective-permute-done | bytes 229408 | tf_op jit(solution)/shard_map/ppermute | solution.py:16
  38.4 3.7 collective-permute-start.7
  42.1 9.3 %collective-permute-done.4 = bf16[128,896]{0,1:T(8,128)(2,1)} collective-permute-done((bf16[128,896]{0,1:T(8,128)(2,1)S(1)}, bf16[128,896]{0,1:T(8,128)(2,1)}, u32[]{:S(2)}, u32[]{:S(2)}) %collective-permute-start.4) | collective-permute-done | bytes 229408 | tf_op jit(solution)/shard_map/ppermute | solution.py:16
  52.1 4.8 %collective-permute-start.8 = (bf16[128,896]{0,1:T(8,128)(2,1)}, bf16[128,896]{0,1:T(8,128)(2,1)S(1)}, u32[]{:S(2)}, u32[]{:S(2)}) collective-permute-start(bf16[128,896]{0,1:T(8,128)(2,1)} %collective-permute-done.7), channel_id=1, source_target_pairs={{0,28},{4,0},{8,4},{12,8},{16,12},{20,16},{24,20},{28,24},{1,29},{... | collective-permute-start | bytes 688136 | tf_op jit(solution)/shard_map/ppermute | solution.py:18
  58.0 5.9 %collective-permute-done.5 = bf16[128,896]{0,1:T(8,128)(2,1)} collective-permute-done((bf16[128,896]{0,1:T(8,128)(2,1)}, bf16[128,896]{0,1:T(8,128)(2,1)}, u32[]{:S(2)}, u32[]{:S(2)}) %collective-permute-start.5) | collective-permute-done | bytes 229408 | tf_op jit(solution)/shard_map/ppermute | solution.py:16
  76.3 2.9 convolution_bitcast_fusion.3
  83.0 2.6 exponential_reduce_fusion.1
  106.7 12.6 %collective-permute-done.10 = bf16[1,256,1024]{2,1,0:T(8,128)(2,1)S(1)} collective-permute-done((bf16[1,256,1024]{2,1,0:T(8,128)(2,1)S(1)}, bf16[1,256,1024]{2,1,0:T(8,128)(2,1)S(1)}, u32[]{:S(2)}, u32[]{:S(2)}) %collective-permute-start.10) | collective-permute-done | bytes 524320 | tf_op jit(solution)/shard_map/ppermute | solution.py:141
  121.2 11.8 %collective-permute-done.11 = bf16[1,256,1024]{2,1,0:T(8,128)(2,1)S(1)} collective-permute-done((bf16[1,256,1024]{2,1,0:T(8,128)(2,1)S(1)}, bf16[1,256,1024]{2,1,0:T(8,128)(2,1)S(1)}, u32[]{:S(2)}, u32[]{:S(2)}) %collective-permute-start.11) | collective-permute-done | bytes 524320 | tf_op jit(solution)/shard_map/ppermute | solution.py:141
  135.2 13.0 %collective-permute-done.16 = bf16[1,256,1024]{2,1,0:T(8,128)(2,1)S(1)} collective-permute-done((bf16[1,256,1024]{2,1,0:T(8,128)(2,1)S(1)}, bf16[1,256,1024]{2,1,0:T(8,128)(2,1)S(1)}, u32[]{:S(2)}, u32[]{:S(2)}) %collective-permute-start.16) | collective-permute-done | bytes 524320 | tf_op jit(solution)/shard_map/ppermute | solution.py:141
  149.5 11.6 %fusion.36 = f32[1024,2304]{1,0:T(8,128)} fusion(bf16[1024,2304]{1,0:T(8,128)(2,1)} %all-gather.3.cloned.1.call-done, bf16[1,512,1024]{2,1,0:T(8,128)(2,1)} %collective-permute-done.12, bf16[1,256,1024]{2,1,0:T(8,128)(2,1)} %copy-done.46, bf16[1,256,1024]{2,1,0:T(8,128)(2,1)S(1)} %multiply_convert_fusion.4), kind=kOutput, calls=%fused_computation.111 | convolution fusion | flops 4838129664 | bytes 16252928 | tf_op jit(solution)/shard_map/dot_general | solution.py:300
  162.8 9.3 %fusion.6 = (bf16[1024,1152]{1,0:T(8,128)(2,1)S(1)}, bf16[1024,1152]{1,0:T(8,128)(2,1)S(1)}, bf16[1024,1152]{1,0:T(8,128)(2,1)S(1)}) fusion(f32[1024,2304]{1,0:T(8,128)} %fusion.36, bf16[1024,1152]{0,1:T(8,128)(2,1)} %all-gather.5.cloned.1.call-done, bf16[1,512,1024]{2,1,0:T(8,128)(2,1)} %collective-permute-done.17, bf16[1,256,1024]{2,1,0:T(8,128)(2,1)} %copy-done.50, ...), kind=kOutput, calls=%fused_computation.18 | convolution fusion | flops 2441084928 | bytes 20971520 | tf_op jit(solution)/shard_map/dot_general | solution.py:303
  172.1 5.1 %fusion.12 = f32[1,1024,1024]{2,1,0:T(8,128)S(1)} fusion(bf16[1024,2304]{1,0:T(8,128)(2,1)S(1)} %copy-done.61, bf16[1024,1152]{1,0:T(8,128)(2,1)S(1)} %get-tuple-element.34, bf16[1024,1152]{1,0:T(8,128)(2,1)S(1)} %get-tuple-element.33), kind=kOutput, calls=%fused_computation.29 | convolution fusion | flops 4841275392 | bytes 13631488 | tf_op jit(solution)/shard_map/dot_general | solution.py:62
  177.4 2.6 collective-permute-done.18
  182.0 12.5 %collective-permute-done.19 = bf16[1,256,1024]{2,1,0:T(8,128)(2,1)S(1)} collective-permute-done((bf16[1,256,1024]{2,1,0:T(8,128)(2,1)S(1)}, bf16[1,256,1024]{2,1,0:T(8,128)(2,1)S(1)}, u32[]{:S(2)}, u32[]{:S(2)}) %collective-permute-start.19) | collective-permute-done | bytes 524320 | tf_op jit(solution)/shard_map/ppermute | solution.py:141
  197.7 11.6 %collective-permute-done.20 = bf16[1,256,1024]{2,1,0:T(8,128)(2,1)S(1)} collective-permute-done((bf16[1,256,1024]{2,1,0:T(8,128)(2,1)S(1)}, bf16[1,256,1024]{2,1,0:T(8,128)(2,1)S(1)}, u32[]{:S(2)}, u32[]{:S(2)}) %collective-permute-start.20) | collective-permute-done | bytes 524320 | tf_op jit(solution)/shard_map/ppermute | solution.py:141
  210.6 5.6 %convolution_convert_fusion.1 = bf16[1024,1152]{1,0:T(8,128)(2,1)} fusion(bf16[1024,1152]{1,0:T(8,128)(2,1)S(1)} %get-tuple-element.35, bf16[1,512,1024]{2,1,0:T(8,128)(2,1)} %collective-permute-done.17, bf16[1,256,1024]{2,1,0:T(8,128)(2,1)S(1)} %copy-done.51, bf16[1,256,1024]{2,1,0:T(8,128)(2,1)S(1)} %copy-done.29), kind=kOutput, calls=%fused_computation.27 | convolution fusion | flops 2423390208 | bytes 6815744 | tf_op jit(solution)/shard_map/dot_general | solution.py:62
  219.2 5.5 %multiply_convert_fusion.1 = bf16[4,512,1024]{2,1,0:T(8,128)(2,1)S(1)} fusion(f32[4,512,1024]{2,1,0:T(8,128)} %copy-done.2, f32[4,512]{1,0:T(4,128)S(1)} %bitcast.214, f32[4,512]{1,0:T(4,128)S(1)} %log_add_fusion.1, pred[512,1024]{1,0:T(8,128)(4,1)S(1)} %copy-done.13, bf16[1024,4,64]{0,2,1:T(8,128)(2,1)S(1)} %bitcast.188, ...), kind=kOutput, calls=%fused_computation.1 | convolution fusion | flops 281018368 | bytes 13910016 | tf_op jit(solution)/shard_map/vmap(qhd,khd->hqk)/dot_general | solution.py:112
  224.8 3.5 multiply_convert_fusion
  235.7 3.8 fusion.22
  249.9 2.7 convolution_convert_fusion.2
  253.9 2.6 copy.48
  256.8 10.1 %convolution_convert_fusion = bf16[1024,2304]{1,0:T(8,128)(2,1)} fusion(bf16[1024,1152]{1,0:T(8,128)(2,1)} %copy-done.65, bf16[1024,1152]{1,0:T(8,128)(2,1)} %copy-done.64, bf16[1,512,1024]{2,1,0:T(8,128)(2,1)} %collective-permute-done.12, bf16[1,256,1024]{2,1,0:T(8,128)(2,1)S(1)} %copy-done.47, bf16[1,256,1024]{2,1,0:T(8,128)(2,1)S(1)} %copy-done.27), kind=kOutput, calls=%fused_computation.11 | convolution fusion | flops 4849926144 | bytes 11534336 | tf_op jit(solution)/shard_map/dot_general | solution.py:62
  266.9 5.3 %convolution_bitcast_fusion.2 = f32[1,1024,1024]{2,1,0:T(8,128)S(1)} fusion(bf16[1024,1152]{1,0:T(8,128)(2,1)} %copy-done.66, bf16[1024,1152]{0,1:T(8,128)(2,1)} %all-gather.5.cloned.1.call-done), kind=kOutput, calls=%fused_computation.32 | convolution fusion | flops 2415919104 | bytes 8912896 | tf_op jit(solution)/shard_map/dot_general | solution.py:62
  286.2 12.0 %collective-permute-done.14 = bf16[1,256,1024]{2,1,0:T(8,128)(2,1)S(1)} collective-permute-done((bf16[1,256,1024]{2,1,0:T(8,128)(2,1)S(1)}, bf16[1,256,1024]{2,1,0:T(8,128)(2,1)S(1)}, u32[]{:S(2)}, u32[]{:S(2)}) %collective-permute-start.14) | collective-permute-done | bytes 524320 | tf_op jit(solution)/shard_map/ppermute | solution.py:141
  299.4 9.5 %collective-permute-done.23 = bf16[1,256,1024]{2,1,0:T(8,128)(2,1)S(1)} collective-permute-done((bf16[1,256,1024]{2,1,0:T(8,128)(2,1)S(1)}, bf16[1,256,1024]{2,1,0:T(8,128)(2,1)S(1)}, u32[]{:S(2)}, u32[]{:S(2)}) %collective-permute-start.23) | collective-permute-done | bytes 524320 | tf_op jit(solution)/shard_map/ppermute | solution.py:141
  315.7 41.5 %psum.7 = f32[2176]{0:T(1024)S(1)} all-reduce(f32[2176]{0:T(1024)S(1)} %concatenate.109), channel_id=1, replica_groups=mesh['fsdp'=8,'ctx'=2,'tensor'=2] {'fsdp','ctx','tensor'}, use_global_device_ids=true, to_apply=%region_21.22 | all-reduce | flops 2176 | bytes 17408 | tf_op jit(solution)/shard_map/psum | solution.py:349
  373.2 78.8 %reduce-scatter.6.cloned.1.call-done = bf16[128,2304]{1,0:T(8,128)(2,1)} async-done(((bf16[1024,2304]{1,0:T(8,128)(2,1)}), bf16[128,2304]{1,0:T(8,128)(2,1)}) %reduce-scatter.6.cloned.1.call-update) | async-done | bytes 589840 | tf_op jit(solution)/shard_map/reduce_scatter | solution.py:311
  456.4 6.8 %collective-permute-done.30 = bf16[128,1152]{1,0:T(8,128)(2,1)S(1)} collective-permute-done((bf16[128,1152]{1,0:T(8,128)(2,1)S(1)}, bf16[128,1152]{1,0:T(8,128)(2,1)S(1)}, u32[]{:S(2)}, u32[]{:S(2)}) %collective-permute-start.30) | collective-permute-done | bytes 294944 | tf_op jit(solution)/shard_map/ppermute | solution.py:141
  464.4 3.8 collective-permute-done.29
  (381 shorter events, 134.8 us)
Async XLA Ops:
  7.2 142.2 %all-gather.3.cloned.1.call-start = ((), (), s32[]{:S(2)}) async-start(), calls=%async_computation.3 | async-start | bytes 5308416 | tf_op jit(solution)/shard_map/all_gather | solution.py:256
  11.8 12.8 %collective-permute-start.2 = (bf16[128,896]{0,1:T(8,128)(2,1)S(1)}, bf16[128,896]{0,1:T(8,128)(2,1)S(1)}, u32[]{:S(2)}, u32[]{:S(2)}) collective-permute-start(bf16[128,896]{0,1:T(8,128)(2,1)S(1)} %constant_dynamic-update-slice_fusion), channel_id=1, source_target_pairs={{0,4},{4,8},{8,12},{12,16},{16,20},{20,24},{24,28},{28,0},{1,5},{5... | collective-permute-start | bytes 688136 | tf_op jit(solution)/shard_map/ppermute | solution.py:16
  14.8 23.6 %collective-permute-start.6 = (bf16[128,896]{0,1:T(8,128)(2,1)S(1)}, bf16[128,896]{0,1:T(8,128)(2,1)S(1)}, u32[]{:S(2)}, u32[]{:S(2)}) collective-permute-start(bf16[128,896]{0,1:T(8,128)(2,1)S(1)} %constant_dynamic-update-slice_fusion), channel_id=1, source_target_pairs={{0,28},{4,0},{8,4},{12,8},{16,12},{20,16},{24,20},{28,24},{1,29},{... | collective-permute-start | bytes 688136 | tf_op jit(solution)/shard_map/ppermute | solution.py:18
  19.1 37.7 %collective-permute-start = (bf16[1,256,1024]{2,1,0:T(8,128)(2,1)S(1)}, bf16[1,256,1024]{2,1,0:T(8,128)(2,1)S(1)}, u32[]{:S(2)}, u32[]{:S(2)}) collective-permute-start(bf16[1,256,1024]{2,1,0:T(8,128)(2,1)S(1)} %get-tuple-element.28), channel_id=1, source_target_pairs={{0,2},{2,0},{1,3},{3,1},{4,6},{6,4},{5,7},{7,5},{8,10},{10,8},{9,1... | collective-permute-start | bytes 1572872 | tf_op jit(solution)/shard_map/ppermute | solution.py:141
  22.7 140.1 %all-gather.5.cloned.1.call-start = ((), (), s32[]{:S(2)}) async-start(), calls=%async_computation.4 | async-start | bytes 2654208 | tf_op jit(solution)/shard_map/all_gather | solution.py:257
  24.6 11.1 %collective-permute-start.3 = (bf16[128,896]{0,1:T(8,128)(2,1)S(1)}, bf16[128,896]{0,1:T(8,128)(2,1)S(1)}, u32[]{:S(2)}, u32[]{:S(2)}) collective-permute-start(bf16[128,896]{0,1:T(8,128)(2,1)S(1)} %collective-permute-done.2), channel_id=1, source_target_pairs={{0,4},{4,8},{8,12},{12,16},{16,20},{20,24},{24,28},{28,0},{1,5},{5... | collective-permute-start | bytes 688136 | tf_op jit(solution)/shard_map/ppermute | solution.py:16
  35.7 15.7 %collective-permute-start.4 = (bf16[128,896]{0,1:T(8,128)(2,1)S(1)}, bf16[128,896]{0,1:T(8,128)(2,1)}, u32[]{:S(2)}, u32[]{:S(2)}) collective-permute-start(bf16[128,896]{0,1:T(8,128)(2,1)S(1)} %collective-permute-done.3), channel_id=1, source_target_pairs={{0,4},{4,8},{8,12},{12,16},{16,20},{20,24},{24,28},{28,0},{1,5},{5... | collective-permute-start | bytes 688136 | tf_op jit(solution)/shard_map/ppermute | solution.py:16
  38.4 13.6 %collective-permute-start.7 = (bf16[128,896]{0,1:T(8,128)(2,1)S(1)}, bf16[128,896]{0,1:T(8,128)(2,1)}, u32[]{:S(2)}, u32[]{:S(2)}) collective-permute-start(bf16[128,896]{0,1:T(8,128)(2,1)S(1)} %collective-permute-done.6), channel_id=1, source_target_pairs={{0,28},{4,0},{8,4},{12,8},{16,12},{20,16},{24,20},{28,24},{1,29},{... | collective-permute-start | bytes 688136 | tf_op jit(solution)/shard_map/ppermute | solution.py:18
  51.5 12.4 %collective-permute-start.5 = (bf16[128,896]{0,1:T(8,128)(2,1)}, bf16[128,896]{0,1:T(8,128)(2,1)}, u32[]{:S(2)}, u32[]{:S(2)}) collective-permute-start(bf16[128,896]{0,1:T(8,128)(2,1)} %collective-permute-done.4), channel_id=1, source_target_pairs={{0,4},{4,8},{8,12},{12,16},{16,20},{20,24},{24,28},{28,0},{1,5},{5... | collective-permute-start | bytes 688136 | tf_op jit(solution)/shard_map/ppermute | solution.py:16
  52.1 16.9 %collective-permute-start.8 = (bf16[128,896]{0,1:T(8,128)(2,1)}, bf16[128,896]{0,1:T(8,128)(2,1)S(1)}, u32[]{:S(2)}, u32[]{:S(2)}) collective-permute-start(bf16[128,896]{0,1:T(8,128)(2,1)} %collective-permute-done.7), channel_id=1, source_target_pairs={{0,28},{4,0},{8,4},{12,8},{16,12},{20,16},{24,20},{28,24},{1,29},{... | collective-permute-start | bytes 688136 | tf_op jit(solution)/shard_map/ppermute | solution.py:18
  58.0 16.6 %collective-permute-start.1 = (bf16[1,512,1024]{2,1,0:T(8,128)(2,1)}, bf16[1,512,1024]{2,1,0:T(8,128)(2,1)}, u32[]{:S(2)}, u32[]{:S(2)}) collective-permute-start(bf16[1,512,1024]{2,1,0:T(8,128)(2,1)} %pad_maximum_fusion.6), channel_id=1, source_target_pairs={{0,1},{1,0},{2,3},{3,2},{4,5},{5,4},{6,7},{7,6},{8,9},{9,8},{10,11... | collective-permute-start | bytes 3145736 | tf_op jit(solution)/shard_map/ppermute | solution.py:141
  101.2 211.7 %reduce-scatter.8.cloned.1.call-start = ((), (), s32[]{:S(2)}) async-start(), calls=%async_computation.6 | async-start | bytes 2654208 | tf_op jit(solution)/shard_map/reduce_scatter | solution.py:309
  105.3 14.0 %collective-permute-start.10 = (bf16[1,256,1024]{2,1,0:T(8,128)(2,1)S(1)}, bf16[1,256,1024]{2,1,0:T(8,128)(2,1)S(1)}, u32[]{:S(2)}, u32[]{:S(2)}) collective-permute-start(bf16[1,256,1024]{2,1,0:T(8,128)(2,1)S(1)} %slice.347), channel_id=1, source_target_pairs={{0,2},{2,0},{1,3},{3,1},{4,6},{6,4},{5,7},{7,5},{8,10},{10,8},{9,1... | collective-permute-start | bytes 1572872 | tf_op jit(solution)/shard_map/ppermute | solution.py:141
  119.8 13.2 %collective-permute-start.11 = (bf16[1,256,1024]{2,1,0:T(8,128)(2,1)S(1)}, bf16[1,256,1024]{2,1,0:T(8,128)(2,1)S(1)}, u32[]{:S(2)}, u32[]{:S(2)}) collective-permute-start(bf16[1,256,1024]{2,1,0:T(8,128)(2,1)S(1)} %multiply_convert_fusion.4), channel_id=1, source_target_pairs={{0,2},{2,0},{1,3},{3,1},{4,6},{6,4},{5,7},{7,5},{8,10},{10,8},{9,1... | collective-permute-start | bytes 1572872 | tf_op jit(solution)/shard_map/ppermute | solution.py:141
  133.8 15.7 %collective-permute-start.12 = (bf16[1,512,1024]{2,1,0:T(8,128)(2,1)S(1)}, bf16[1,512,1024]{2,1,0:T(8,128)(2,1)}, u32[]{:S(2)}, u32[]{:S(2)}) collective-permute-start(bf16[1,512,1024]{2,1,0:T(8,128)(2,1)S(1)} %pad_maximum_fusion.7), channel_id=1, source_target_pairs={{0,1},{1,0},{2,3},{3,2},{4,5},{5,4},{6,7},{7,6},{8,9},{9,8},{10,11... | collective-permute-start | bytes 3145736 | tf_op jit(solution)/shard_map/ppermute | solution.py:141
  133.8 14.4 %collective-permute-start.16 = (bf16[1,256,1024]{2,1,0:T(8,128)(2,1)S(1)}, bf16[1,256,1024]{2,1,0:T(8,128)(2,1)S(1)}, u32[]{:S(2)}, u32[]{:S(2)}) collective-permute-start(bf16[1,256,1024]{2,1,0:T(8,128)(2,1)S(1)} %constant_dynamic-slice_fusion), channel_id=1, source_target_pairs={{0,2},{2,0},{1,3},{3,1},{4,6},{6,4},{5,7},{7,5},{8,10},{10,8},{9,1... | collective-permute-start | bytes 1572872 | tf_op jit(solution)/shard_map/ppermute | solution.py:141
  149.4 11.6 %collective-permute-start.17 = (bf16[1,512,1024]{2,1,0:T(8,128)(2,1)}, bf16[1,512,1024]{2,1,0:T(8,128)(2,1)}, u32[]{:S(2)}, u32[]{:S(2)}) collective-permute-start(bf16[1,512,1024]{2,1,0:T(8,128)(2,1)} %pad_maximum_fusion.8), channel_id=1, source_target_pairs={{0,1},{1,0},{2,3},{3,2},{4,5},{5,4},{6,7},{7,6},{8,9},{9,8},{10,11... | collective-permute-start | bytes 3145736 | tf_op jit(solution)/shard_map/ppermute | solution.py:141
  180.5 14.0 %collective-permute-start.19 = (bf16[1,256,1024]{2,1,0:T(8,128)(2,1)S(1)}, bf16[1,256,1024]{2,1,0:T(8,128)(2,1)S(1)}, u32[]{:S(2)}, u32[]{:S(2)}) collective-permute-start(bf16[1,256,1024]{2,1,0:T(8,128)(2,1)S(1)} %slice.345), channel_id=1, source_target_pairs={{0,2},{2,0},{1,3},{3,1},{4,6},{6,4},{5,7},{7,5},{8,10},{10,8},{9,1... | collective-permute-start | bytes 1572872 | tf_op jit(solution)/shard_map/ppermute | solution.py:141
  196.2 13.1 %collective-permute-start.20 = (bf16[1,256,1024]{2,1,0:T(8,128)(2,1)S(1)}, bf16[1,256,1024]{2,1,0:T(8,128)(2,1)S(1)}, u32[]{:S(2)}, u32[]{:S(2)}) collective-permute-start(bf16[1,256,1024]{2,1,0:T(8,128)(2,1)S(1)} %get-tuple-element.25), channel_id=1, source_target_pairs={{0,2},{2,0},{1,3},{3,1},{4,6},{6,4},{5,7},{7,5},{8,10},{10,8},{9,1... | collective-permute-start | bytes 1572872 | tf_op jit(solution)/shard_map/ppermute | solution.py:141
  210.6 5.8 %collective-permute-start.21 = (bf16[1,512,1024]{2,1,0:T(8,128)(2,1)}, bf16[1,512,1024]{2,1,0:T(8,128)(2,1)}, u32[]{:S(2)}, u32[]{:S(2)}) collective-permute-start(bf16[1,512,1024]{2,1,0:T(8,128)(2,1)} %pad_maximum_fusion.9), channel_id=1, source_target_pairs={{0,1},{1,0},{2,3},{3,2},{4,5},{5,4},{6,7},{7,6},{8,9},{9,8},{10,11... | collective-permute-start | bytes 3145736 | tf_op jit(solution)/shard_map/ppermute | solution.py:141
  216.3 144.9 %reduce-scatter.10.cloned.1.call-start = ((), (), s32[]{:S(2)}) async-start(), calls=%async_computation.7 | async-start | bytes 1769472
  256.5 195.5 %reduce-scatter.6.cloned.1.call-start = ((), (), s32[]{:S(2)}) async-start(), calls=%async_computation.5 | async-start | bytes 5308416 | tf_op jit(solution)/shard_map/reduce_scatter | solution.py:311
  274.6 6.3 %collective-permute-start.13 = (bf16[1,512,1024]{2,1,0:T(8,128)(2,1)}, bf16[1,512,1024]{2,1,0:T(8,128)(2,1)}, u32[]{:S(2)}, u32[]{:S(2)}) collective-permute-start(bf16[1,512,1024]{2,1,0:T(8,128)(2,1)} %slice.342), channel_id=1, source_target_pairs={{0,1},{1,0},{2,3},{3,2},{4,5},{5,4},{6,7},{7,6},{8,9},{9,8},{10,11... | collective-permute-start | bytes 3145736 | tf_op jit(solution)/shard_map/ppermute | solution.py:141
  283.3 14.9 %collective-permute-start.14 = (bf16[1,256,1024]{2,1,0:T(8,128)(2,1)S(1)}, bf16[1,256,1024]{2,1,0:T(8,128)(2,1)S(1)}, u32[]{:S(2)}, u32[]{:S(2)}) collective-permute-start(bf16[1,256,1024]{2,1,0:T(8,128)(2,1)S(1)} %slice.346), channel_id=1, source_target_pairs={{0,2},{2,0},{1,3},{3,1},{4,6},{6,4},{5,7},{7,5},{8,10},{10,8},{9,1... | collective-permute-start | bytes 1572872 | tf_op jit(solution)/shard_map/ppermute | solution.py:141
  285.4 23.5 %collective-permute-start.23 = (bf16[1,256,1024]{2,1,0:T(8,128)(2,1)S(1)}, bf16[1,256,1024]{2,1,0:T(8,128)(2,1)S(1)}, u32[]{:S(2)}, u32[]{:S(2)}) collective-permute-start(bf16[1,256,1024]{2,1,0:T(8,128)(2,1)S(1)} %slice.344), channel_id=1, source_target_pairs={{0,2},{2,0},{1,3},{3,1},{4,6},{6,4},{5,7},{7,5},{8,10},{10,8},{9,1... | collective-permute-start | bytes 1572872 | tf_op jit(solution)/shard_map/ppermute | solution.py:141
  299.4 11.6 %collective-permute-start.15 = (bf16[1,256,1024]{2,1,0:T(8,128)(2,1)}, bf16[1,256,1024]{2,1,0:T(8,128)(2,1)}, u32[]{:S(2)}, u32[]{:S(2)}) collective-permute-start(bf16[1,256,1024]{2,1,0:T(8,128)(2,1)} %get-tuple-element.30), channel_id=1, source_target_pairs={{0,1},{1,0},{2,3},{3,2},{4,5},{5,4},{6,7},{7,6},{8,9},{9,8},{10,11... | collective-permute-start | bytes 1572872 | tf_op jit(solution)/shard_map/ppermute | solution.py:141
  311.0 48.8 %collective-permute-start.24 = (f32[1,256,1024]{2,1,0:T(8,128)}, f32[1,256,1024]{2,1,0:T(8,128)}, u32[]{:S(2)}, u32[]{:S(2)}) collective-permute-start(f32[1,256,1024]{2,1,0:T(8,128)} %get-tuple-element.24), channel_id=1, source_target_pairs={{0,1},{1,0},{2,3},{3,2},{4,5},{5,4},{6,7},{7,6},{8,9},{9,8},{10,11... | collective-permute-start | bytes 3145736 | tf_op jit(solution)/shard_map/ppermute | solution.py:141
  314.1 44.4 %collective-permute-start.31 = (bf16[1152,128]{0,1:T(8,128)(2,1)}, bf16[1152,128]{0,1:T(8,128)(2,1)S(1)}, u32[]{:S(2)}, u32[]{:S(2)}) collective-permute-start(bf16[1152,128]{0,1:T(8,128)(2,1)} %bitcast.198), channel_id=1, source_target_pairs={{0,2},{2,0},{1,3},{3,1},{4,6},{6,4},{5,7},{7,5},{8,10},{10,8},{9,1... | collective-permute-start | bytes 884744 | tf_op jit(solution)/shard_map/ppermute | solution.py:141
  362.4 8.9 %collective-permute-start.28 = (bf16[256,128]{1,0:T(8,128)(2,1)S(1)}, bf16[256,128]{1,0:T(8,128)(2,1)S(1)}, u32[]{:S(2)}, u32[]{:S(2)}) collective-permute-start(bf16[256,128]{1,0:T(8,128)(2,1)S(1)} %bitcast.201), channel_id=1, source_target_pairs={{0,2},{2,0},{1,3},{3,1},{4,6},{6,4},{5,7},{7,5},{8,10},{10,8},{9,1... | collective-permute-start | bytes 196616 | tf_op jit(solution)/shard_map/ppermute | solution.py:141
  365.9 4.5 collective-permute-start.26
  453.3 9.9 %collective-permute-start.30 = (bf16[128,1152]{1,0:T(8,128)(2,1)S(1)}, bf16[128,1152]{1,0:T(8,128)(2,1)S(1)}, u32[]{:S(2)}, u32[]{:S(2)}) collective-permute-start(bf16[128,1152]{1,0:T(8,128)(2,1)S(1)} %get-tuple-element.44), channel_id=1, source_target_pairs={{0,2},{2,0},{1,3},{3,1},{4,6},{6,4},{5,7},{7,5},{8,10},{10,8},{9,1... | collective-permute-start | bytes 884744 | tf_op jit(solution)/shard_map/ppermute | solution.py:141
  454.8 13.3 %collective-permute-start.29 = (bf16[128,1152]{1,0:T(8,128)(2,1)S(1)}, bf16[128,1152]{1,0:T(8,128)(2,1)S(1)}, u32[]{:S(2)}, u32[]{:S(2)}) collective-permute-start(bf16[128,1152]{1,0:T(8,128)(2,1)S(1)} %get-tuple-element.46), channel_id=1, source_target_pairs={{0,2},{2,0},{1,3},{3,1},{4,6},{6,4},{5,7},{7,5},{8,10},{10,8},{9,1... | collective-permute-start | bytes 884744 | tf_op jit(solution)/shard_map/ppermute | solution.py:141
  (78 other events, 850.7 us)
Sparse Core Ops, SparseCore 0:
  22.8 86.2 all-gather.2
  111.1 51.6 all-gather.4
  216.4 69.2 reduce-scatter.7
  289.0 64.9 reduce-scatter.9
  357.5 94.5 reduce-scatter.5
